TPU v7x, 128 devices: a whole 4x4x4 slice. The times are simulated.
128 devices in a mesh: grp: 4 (over x_hi, core), sub: 32 (over x_lo, y, z).
Axes of the slice: x: 4 (x_hi: 2, x_lo: 2; x = x_hi * 2 + x_lo), y: 4, z: 4, core: 2. Of those that a mesh axis runs over, the one named last changes fastest.
Arguments:
- template: bfloat16 [96, 96, 128], P('sub'), may hold values from -4 to 4
- subjects: bfloat16 [128, 96, 96, 128], P(('grp', 'sub')), may hold values from -40 to 40
Outputs:
- velocity: float32 [96, 3, 96, 128], P('sub')
- new_template: float32 [96, 96, 128], P('sub')
- similarity: float32 [], replicated
All inputs are finite; a program needn't handle non-finite values.
Results may differ from a plain program's by a relative error of at most 0.0003.
Values may be sent and summed in bfloat16 or wider, within the bound.
No kernel may reach another device: no remote copies, remote signals or barrier semaphores. Data moves between devices by JAX's collectives and lax.ppermute only.
A program may use at most 128 MiB of HBM per device.

v0:
```python
import math
import jax
import jax.numpy as jnp
from jax import lax
from jax.sharding import PartitionSpec as P

RADIUS = 4
REACH = 5
EPSILON = 1e-05
STEP_LENGTH = 0.5
VARIANCE = 3.0
HIGH = lax.Precision.HIGHEST


def padded_2(x, sides, width):
    for axis, dim in sides:
        devices, length = (lax.axis_size(axis), x.shape[dim])
        up = [(i, (i + 1) % devices) for i in range(devices - 1)]
        down = [(j, i) for i, j in up]
        last = lax.slice_in_dim(x, length - width, length, axis=dim)
        initial = lax.slice_in_dim(x, 0, width, axis=dim)
        before = lax.ppermute(last, axis, up)
        after = lax.ppermute(initial, axis, down)
        x = jnp.concatenate([before, x, after], axis=dim)
    return x


def band_matrix(length, extent, weighted):
    row_ids = lax.broadcasted_iota(jnp.int32, (length, length), 0)
    col_ids = lax.broadcasted_iota(jnp.int32, (length, length), 1)
    inside = jnp.abs(row_ids - col_ids) <= extent
    if weighted:
        kernel_sum = sum(
            (math.exp(-offset * offset / (2.0 * VARIANCE)) for offset in range(-extent, extent + 1))
        )
        offset_f = (row_ids - col_ids).astype(jnp.float32)
        values = jnp.exp(-offset_f * offset_f / (2.0 * VARIANCE)) / kernel_sum
        return jnp.where(inside, values, 0.0)
    return jnp.where(inside, 1.0 / (2 * extent + 1), 0.0).astype(jnp.float32)


def filter_volume(volume, along_z, along_x, along_y):
    result = jnp.dot(volume, along_y, precision=HIGH, preferred_element_type=jnp.float32)
    result = jnp.einsum(
        "ab,zby->zay", along_x, result, precision=HIGH, preferred_element_type=jnp.float32
    )
    return jnp.einsum(
        "ab,bxy->axy", along_z, result, precision=HIGH, preferred_element_type=jnp.float32
    )


def central(volume):
    padded = jnp.pad(volume, 1)
    along_z = (padded[2:, 1:-1, 1:-1] - padded[:-2, 1:-1, 1:-1]) * 0.5
    along_x = (padded[1:-1, 2:, 1:-1] - padded[1:-1, :-2, 1:-1]) * 0.5
    along_y = (padded[1:-1, 1:-1, 2:] - padded[1:-1, 1:-1, :-2]) * 0.5
    return jnp.stack([along_z, along_x, along_y], axis=1)


def on_device(template, subjects):
    fixed_image = lax.all_gather(template, "sub", axis=0, tiled=True).astype(jnp.float32)
    depth, height, width = fixed_image.shape
    box_z = band_matrix(depth, RADIUS, False)
    box_x = band_matrix(height, RADIUS, False)
    box_y = band_matrix(width, RADIUS, False)
    gauss_z = band_matrix(depth, REACH, True)
    gauss_x = band_matrix(height, REACH, True)
    gauss_y = band_matrix(width, REACH, True)
    mean_i = filter_volume(fixed_image, box_z, box_x, box_y)
    mean_ii = filter_volume(fixed_image * fixed_image, box_z, box_x, box_y)
    var_i = mean_ii - mean_i * mean_i
    centred_i = fixed_image - mean_i
    gradients = central(fixed_image)
    moving = subjects[0].astype(jnp.float32)
    mean_j = filter_volume(moving, box_z, box_x, box_y)
    mean_jj = filter_volume(moving * moving, box_z, box_x, box_y)
    mean_ij = filter_volume(fixed_image * moving, box_z, box_x, box_y)
    cross_sum = mean_ij - mean_i * mean_j
    var_j = mean_jj - mean_j * mean_j
    denominator = var_i * var_j + EPSILON
    factor = (
        2.0
        * cross_sum
        / denominator
        * (moving - mean_j - cross_sum / (var_i + EPSILON) * centred_i)
    )
    force_total = factor[:, None] * gradients
    cc_local = jnp.sum(cross_sum * cross_sum / denominator)
    planar = jnp.einsum(
        "zcxb,ba->zcxa", force_total, gauss_y, precision=HIGH, preferred_element_type=jnp.float32
    )
    planar = jnp.einsum(
        "ab,zcby->zcay", gauss_x, planar, precision=HIGH, preferred_element_type=jnp.float32
    )
    group_count = lax.axis_size("grp")
    subject_count = subjects.shape[0] * group_count * lax.axis_size("sub")
    smooth = jnp.einsum(
        "ab,bcxy->acxy", gauss_z, planar, precision=HIGH, preferred_element_type=jnp.float32
    )
    intensity = moving[:, None]
    owner_part = lax.psum_scatter(
        jnp.concatenate([smooth, intensity], axis=1), "sub", scatter_dimension=0, tiled=True
    )
    summed = lax.psum(owner_part, "grp")
    mean_velocity = summed[:, :3] / subject_count
    mean_image = summed[:, 3] / subject_count
    padded_mean = padded_2(mean_image, (("sub", 0),), 1)
    velocity_square = jnp.sum(mean_velocity * mean_velocity)
    image_square = jnp.sum(mean_image * mean_image)
    cc_total = lax.psum(cc_local, ("grp", "sub"))
    velocity_total, image_sq_total = lax.psum((velocity_square, image_square), "sub")
    cell_count = depth * height * width
    velocity_norm = jnp.sqrt(velocity_total / cell_count + EPSILON)
    image_norm = jnp.sqrt(image_sq_total / cell_count + EPSILON)
    velocity = STEP_LENGTH * mean_velocity / velocity_norm
    slope_z = (padded_mean[2:] - padded_mean[:-2]) * 0.5
    padded_x = jnp.pad(mean_image, ((0, 0), (1, 1), (0, 0)))
    slope_x = (padded_x[:, 2:] - padded_x[:, :-2]) * 0.5
    padded_y = jnp.pad(mean_image, ((0, 0), (0, 0), (1, 1)))
    slope_y = (padded_y[:, :, 2:] - padded_y[:, :, :-2]) * 0.5
    advected = velocity[:, 0] * slope_z + velocity[:, 1] * slope_x + velocity[:, 2] * slope_y
    new_template = (mean_image - advected) / image_norm
    similarity = cc_total / (subject_count * cell_count)
    return (velocity, new_template, similarity)


def solution(mesh):
    placed = (P("sub", None, None), P(("grp", "sub"), None, None, None))
    return jax.shard_map(
        on_device,
        mesh=mesh,
        in_specs=placed,
        out_specs=(P("sub", None, None, None), P("sub", None, None), P()),
        check_vma=False,
    )
```

profile of v0, /device:TPU:2, one launch (start us, length us, event | category | flops | bytes accessed | tf_op | source)
XLA Modules:
  0.0 771.6 jit_solution(3366972188630262749)
XLA Ops:
  13.9 6.3 copy.25
  20.1 9.0 %convolution_bitcast_fusion.1 = f32[96,96,128]{1,0,2:T(8,128)} fusion(f32[96,96,128]{1,0,2:T(8,128)} %copy.25), kind=kOutput, calls=%fused_computation.45 | convolution fusion | flops 1358991360 | bytes 9437184 | tf_op jit(solution)/shard_map/ab,zby->zay/dot_general | solution.py:44
  29.1 6.4 copy.26
  45.3 118.9 %all-gather.2.cloned.1.call-done = bf16[96,96,128]{2,1,0:T(8,128)(2,1)} async-done(((bf16[3,96,128]{2,1,0:T(8,128)(2,1)}), bf16[96,96,128]{2,1,0:T(8,128)(2,1)}) %all-gather.2.cloned.1.call-update) | async-done | bytes 2359312 | tf_op jit(solution)/shard_map/all_gather | solution.py:61
  168.1 7.6 fusion.17
  180.8 9.9 %fusion.15 = f32[96,96,128]{2,0,1:T(8,128)} fusion(f32[96,96,128]{2,1,0:T(8,128)S(1)} %convolution_bitcast_fusion.3), kind=kOutput, calls=%fused_computation.27 | convolution fusion | flops 1358991360 | bytes 9437184 | tf_op jit(solution)/shard_map/ab,bxy->axy/dot_general | solution.py:47
  190.7 7.6 fusion.21
  203.2 9.9 %fusion.19 = f32[96,96,128]{2,0,1:T(8,128)} fusion(f32[96,96,128]{2,1,0:T(8,128)S(1)} %convolution_bitcast_fusion.4), kind=kOutput, calls=%fused_computation.31 | convolution fusion | flops 1358991360 | bytes 9437184 | tf_op jit(solution)/shard_map/ab,bxy->axy/dot_general | solution.py:47
  213.1 7.6 fusion.25
  220.6 6.1 convolution_bitcast_fusion.6
  230.4 6.3 copy.22
  236.7 9.0 %convolution_bitcast_fusion.2 = f32[96,96,128]{1,0,2:T(8,128)} fusion(f32[96,96,128]{1,0,2:T(8,128)} %copy.22), kind=kOutput, calls=%fused_computation.46 | convolution fusion | flops 1358991360 | bytes 9437184 | tf_op jit(solution)/shard_map/ab,zby->zay/dot_general | solution.py:44
  245.7 6.3 copy.23
  251.9 8.8 %fusion.84 = f32[96,96,128]{2,0,1:T(8,128)} fusion(f32[96,96,128]{2,0,1:T(8,128)} %copy.23), kind=kOutput, calls=%fused_computation.118 | convolution fusion | flops 1358991360 | bytes 9437184 | tf_op jit(solution)/shard_map/ab,bxy->axy/dot_general | solution.py:47
  261.5 7.5 fusion.8
  269.0 21.9 %fusion.27 = (f32[]{:T(128)}, f32[96,96,128]{2,0,1:T(8,128)}) fusion(f32[96,96,128]{2,0,1:T(8,128)} %fusion.84, f32[96,96,128]{2,0,1:T(8,128)} %fusion.81, f32[96,96,128]{2,0,1:T(8,128)} %fusion.15, f32[96,96,128]{2,0,1:T(8,128)} %fusion.19, bf16[96,96,128]{2,1,0:T(8,128)(2,1)S(1)} %copy-done.2, bf16[1,96,96,128]{3,2,1,0:T(8,128)(2,1)S(1)} %copy-done, ...), kind=kOutput, calls=%fused_computation.43 | convolution fusion | flops 1384943616 | bytes 33030148 | tf_op jit(solution)/shard_map/ab,bxy->axy/dot_general | solution.py:47
  296.1 22.1 %fusion.2 = f32[96,3,96,128]{3,2,1,0:T(8,128)S(1)} fusion(f32[96,3,96,128]{3,0,2,1:T(8,128)S(1)} %maximum_multiply_fusion), kind=kOutput, calls=%fused_computation.10 | convolution fusion | flops 5435965440 | bytes 28311552 | tf_op jit(solution)/shard_map/zcxb,ba->zcxa/dot_general | solution.py:89
  318.2 15.9 %convolution_bitcast_fusion = f32[96,3,96,128]{3,2,1,0:T(8,128)} fusion(f32[96,3,96,128]{3,2,1,0:T(8,128)S(1)} %fusion.2), kind=kOutput, calls=%fused_computation.12 | convolution fusion | flops 4076946432 | bytes 28311552 | tf_op jit(solution)/shard_map/ab,zcby->zcay/dot_general | solution.py:92
  334.1 25.3 %fusion = f32[96,3,96,128]{3,0,2,1:T(8,128)S(1)} fusion(f32[96,3,96,128]{3,2,1,0:T(8,128)} %convolution_bitcast_fusion), kind=kOutput, calls=%fused_computation.8 | convolution fusion | flops 4076946432 | bytes 28311552 | tf_op jit(solution)/shard_map/ab,bcxy->acxy/dot_general | solution.py:97
  359.5 7.1 pad_maximum_fusion
  366.6 15.8 %copy.34 = f32[96,4,96,128]{3,2,1,0:T(8,128)} copy(f32[96,4,96,128]{3,0,2,1:T(8,128)} %pad_maximum_fusion) | data formatting | bytes 37748736 | tf_op jit(solution)/shard_map/concatenate | solution.py:102
  382.4 218.4 %reduce-scatter.2.cloned.1.call-done = f32[3,4,96,128]{3,2,1,0:T(8,128)} async-done(((f32[96,4,96,128]{3,2,1,0:T(8,128)}), f32[3,4,96,128]{3,2,1,0:T(8,128)}) %reduce-scatter.2.cloned.1.call-update) | async-done | bytes 589840 | tf_op jit(solution)/shard_map/reduce_scatter | solution.py:101
  600.9 64.6 %psum.31 = f32[]{:T(128)} all-reduce(f32[]{:T(128)} %get-tuple-element.14), channel_id=1, replica_groups=mesh['grp'=4,'sub'=32] {'grp','sub'}, use_global_device_ids=true, to_apply=%region_7.8 | all-reduce | flops 1 | bytes 8 | tf_op jit(solution)/shard_map/psum | solution.py:110
  669.4 79.7 %all-reduce.3 = (f32[]{:T(128)}, f32[]{:T(128)}) all-reduce(f32[]{:T(128)} %multiply_reduce_fusion, f32[]{:T(128)} %multiply_reduce_fusion.1), channel_id=1, replica_groups=mesh['grp'=4,'sub'=32] {'sub'}, use_global_device_ids=true, to_apply=%region_3.4 | all-reduce | flops 2 | bytes 16 | tf_op jit(solution)/shard_map/psum | solution.py:111
  (44 shorter events, 56.6 us)
Async XLA Ops:
  7.2 157.0 %all-gather.2.cloned.1.call-start = ((), (), s32[]{:S(2)}) async-start(), calls=%async_computation.1 | async-start | bytes 2433024 | tf_op jit(solution)/shard_map/all_gather | solution.py:61
  7.9 592.9 %reduce-scatter.2.cloned.1.call-start = ((), (), s32[]{:S(2)}) async-start(), calls=%async_computation.2 | async-start | bytes 19464192 | tf_op jit(solution)/shard_map/reduce_scatter | solution.py:101
  29.1 6.4 copy-start
  35.5 3.9 copy-start.3
  220.6 6.2 copy-start.1
  251.9 8.8 %copy-start.2 = (bf16[96,96,128]{2,1,0:T(8,128)(2,1)S(1)}, bf16[96,96,128]{2,1,0:T(8,128)(2,1)}, u32[]{:S(2)}) copy-start(bf16[96,96,128]{2,1,0:T(8,128)(2,1)} %all-gather.2.cloned.1.call-done) | copy-start | bytes 7077892
  269.0 21.9 %copy-start.4 = (f32[96,1,96,128]{3,0,2,1:T(8,128)S(1)}, f32[96,1,96,128]{3,0,2,1:T(8,128)}, u32[]{:S(2)}) copy-start(f32[96,1,96,128]{3,0,2,1:T(8,128)} %get-tuple-element.16) | copy-start | bytes 14155780
  269.0 21.9 %copy-start.5 = (f32[96,1,96,128]{3,0,2,1:T(8,128)S(1)}, f32[96,1,96,128]{3,0,2,1:T(8,128)}, u32[]{:S(2)}) copy-start(f32[96,1,96,128]{3,0,2,1:T(8,128)} %get-tuple-element.17) | copy-start | bytes 14155780
  318.2 41.2 %slice-start = ((s8[4718592]{0:T(1024)(128)(4,1)}), s8[4194304]{0:T(1024)(128)(4,1)S(1)}, s32[]{:S(2)}) async-start(s8[4718592]{0:T(1024)(128)(4,1)} %bitcast.107), calls=%async_computation.4 | async-start | bytes 8388608
  334.1 25.3 %slice-start.1 = ((s8[4718592]{0:T(1024)(128)(4,1)}), s8[524288]{0:T(1024)(128)(4,1)S(1)}, s32[]{:S(2)}) async-start(s8[4718592]{0:T(1024)(128)(4,1)} %bitcast.107), calls=%async_computation.5 | async-start | bytes 1048576
  382.4 283.1 %all-reduce.6.cloned.1.call-start = ((), (), s32[]{:S(2)}) async-start(), calls=%async_computation.3 | async-start | bytes 1179648 | tf_op jit(solution)/shard_map/psum | solution.py:104
  750.7 8.4 %collective-permute-start = (f32[1,96,128]{2,1,0:T(8,128)S(1)}, f32[1,96,128]{2,1,0:T(8,128)S(1)}, u32[]{:S(2)}, u32[]{:S(2)}) collective-permute-start(f32[1,96,128]{2,1,0:T(8,128)S(1)} %get-tuple-element.24), channel_id=1, source_target_pairs={{1,0},{2,1},{3,2},{4,3},{5,4},{6,5},{7,6},{8,7},{9,8},{10,9},{11,1... | collective-permute-start | bytes 147464 | tf_op jit(solution)/shard_map/ppermute | solution.py:23
  752.7 10.2 %collective-permute-start.1 = (f32[1,96,128]{2,1,0:T(8,128)S(1)}, f32[1,96,128]{2,1,0:T(8,128)S(1)}, u32[]{:S(2)}, u32[]{:S(2)}) collective-permute-start(f32[1,96,128]{2,1,0:T(8,128)S(1)} %get-tuple-element.25), channel_id=1, source_target_pairs={{0,1},{1,2},{2,3},{3,4},{4,5},{5,6},{6,7},{7,8},{8,9},{9,10},{10,1... | collective-permute-start | bytes 147464 | tf_op jit(solution)/shard_map/ppermute | solution.py:22
Sparse Core Ops, SparseCore 0:
  9.6 154.5 all-gather.1
  382.5 218.3 reduce-scatter.1
  603.4 40.4 all-reduce.5
where the time goes:
time: 778 us; the launch traced here: 772 us
  waiting for transfers between devices  342 us (44%)
  matrix products  186 us (24%)
  blocking collectives  144 us (19%)
  local copies, waits for them, and re-layouts  42.6 us (5%)
  other arithmetic  33.7 us (4%)
  between operations  17.4 us (2%)
    reduce_scatter x1, waiting for transfers between devices, on_device(): lax.psum_scatter(jnp.concatenate([smooth, intensity], axis=1), 'sub', sca...  218 us
    all_gather x1, waiting for transfers between devices, on_device(): lax.all_gather(template, 'sub', axis=0, tiled=True).astype(jnp.float32)  119 us
    psum x1, blocking collectives, on_device(): lax.psum((velocity_square, image_square), 'sub')  79.7 us
    psum x1, blocking collectives, on_device(): cc_total = lax.psum(cc_local, ('grp', 'sub'))  64.6 us
    dot_general x5, matrix products, filter_volume(): jnp.einsum('ab,bxy->axy', along_z, result, precision=HIGH, preferred_elem...  56.4 us
    dot_general x5, matrix products, filter_volume(): jnp.einsum('ab,zby->zay', along_x, result, precision=HIGH, preferred_elem...  34.1 us
    dot_general x5, matrix products, filter_volume(): jnp.dot(volume, along_y, precision=HIGH, preferred_element_type=jnp.float32)  32.2 us
    dot_general x1, matrix products, on_device(): jnp.einsum('ab,bcxy->acxy', gauss_z, planar, precision=HIGH, preferred_el...  25.3 us
  transfers between devices with their start and end apart: 5, of which 3 were waited for; matrix products, arithmetic and copies ran while one was open for 5% of the time, Pallas kernels for 0%

commit v1 on v0

--- a/solution.py
+++ b/solution.py
@@ -10,6 +10,11 @@
 STEP_LENGTH = 0.5
 VARIANCE = 3.0
 HIGH = lax.Precision.HIGHEST
+
+
+def all_by_exchange(x, name, dim):
+    sent = jnp.stack([x] * lax.axis_size(name))
+    return jnp.concatenate(lax.all_to_all(sent, name, 0, 0), axis=dim)
 
 
 def padded_2(x, sides, width):
@@ -58,7 +63,7 @@
 
 
 def on_device(template, subjects):
-    fixed_image = lax.all_gather(template, "sub", axis=0, tiled=True).astype(jnp.float32)
+    fixed_image = all_by_exchange(template, "sub", 0).astype(jnp.float32)
     depth, height, width = fixed_image.shape
     box_z = band_matrix(depth, RADIUS, False)
     box_x = band_matrix(height, RADIUS, False)

time: 778 us -> 685 us (0.88)
  waiting for transfers between devices: 342 us -> 222 us
  other arithmetic: 33.7 us -> 45.4 us
  starting transfers between devices: 5.96 us -> 15.5 us
    all_gather x1 -> x0, waiting for transfers between devices: 119 us -> none  [on_device(): lax.all_gather(template, 'sub', axis=0, tiled=True).astype(jnp.float32)]
    all_to_all x0 -> x1, starting transfers between devices: none -> 9.57 us  [all_by_exchange(): return jnp.concatenate(lax.all_to_all(sent, name, 0, 0), axis=dim)]
    another operation x1, other arithmetic: 7.52 us -> 15.5 us  [central(): return jnp.stack([along_z, along_x, along_y], axis=1)]
  transfers between devices with their start and end apart: 5 -> 5, of which waited for: 3 -> 2; matrix products, arithmetic and copies ran while one was open for 5% -> 6% of each run, Pallas kernels for 0% -> 0%
where the time goes in v1:
time: 685 us; the launch traced here: 676 us
  waiting for transfers between devices  222 us (32%)
  matrix products  186 us (27%)
  blocking collectives  144 us (21%)
  other arithmetic  45.4 us (7%)
  local copies, waits for them, and re-layouts  44.4 us (6%)
  between operations  17.8 us (3%)
  starting transfers between devices  15.5 us (2%)
    reduce_scatter x1, waiting for transfers between devices, on_device(): lax.psum_scatter(jnp.concatenate([smooth, intensity], axis=1), 'sub', sca...  218 us
    psum x1, blocking collectives, on_device(): lax.psum((velocity_square, image_square), 'sub')  79.7 us
    psum x1, blocking collectives, on_device(): cc_total = lax.psum(cc_local, ('grp', 'sub'))  64.7 us
    dot_general x5, matrix products, filter_volume(): jnp.einsum('ab,bxy->axy', along_z, result, precision=HIGH, preferred_elem...  56.5 us
    dot_general x5, matrix products, filter_volume(): jnp.einsum('ab,zby->zay', along_x, result, precision=HIGH, preferred_elem...  34.1 us
    dot_general x5, matrix products, filter_volume(): jnp.dot(volume, along_y, precision=HIGH, preferred_element_type=jnp.float32)  32.5 us
    dot_general x1, matrix products, on_device(): jnp.einsum('ab,bcxy->acxy', gauss_z, planar, precision=HIGH, preferred_el...  25.3 us
    dot_general x1, matrix products, on_device(): jnp.einsum('zcxb,ba->zcxa', force_total, gauss_y, precision=HIGH, preferr...  22.1 us
  transfers between devices with their start and end apart: 5, of which 2 were waited for; matrix products, arithmetic and copies ran while one was open for 6% of the time, Pallas kernels for 0%

profile of v1, /device:TPU:2, one launch (start us, length us, event | category | flops | bytes accessed | tf_op | source)
XLA Modules:
  0.0 675.6 jit_solution(14704381296583876196)
XLA Ops:
  9.8 9.6 %all-to-all-start = ((bf16[32,3,96,128]{3,2,1,0:T(8,128)(2,1)}), bf16[32,3,96,128]{3,2,1,0:T(8,128)(2,1)S(1)}, u32[]{:S(2)}, u32[]{:S(2)}) async-start(bf16[32,3,96,128]{3,2,1,0:T(8,128)(2,1)} %stack.10), calls=%async_computation | async-start | bytes 4718592 | tf_op jit(solution)/shard_map/all_to_all | solution.py:17
  25.3 6.3 copy.26
  31.6 9.0 %convolution_bitcast_fusion.1 = f32[96,96,128]{1,0,2:T(8,128)} fusion(f32[96,96,128]{1,0,2:T(8,128)} %copy.26), kind=kOutput, calls=%fused_computation.45 | convolution fusion | flops 1358991360 | bytes 9437184 | tf_op jit(solution)/shard_map/ab,zby->zay/dot_general | solution.py:49
  40.6 6.3 copy.27
  68.0 7.6 %fusion.17 = f32[96,96,128]{2,1,0:T(8,128)S(1)} fusion(f32[96,96,128]{2,0,1:T(8,128)S(1)} %get-tuple-element.19), kind=kOutput, calls=%fused_computation.29 | convolution fusion | flops 1812004864 | bytes 9437184 | tf_op jit(solution)/shard_map/dot_general | solution.py:48
  80.7 9.9 %fusion.15 = f32[96,96,128]{2,0,1:T(8,128)} fusion(f32[96,96,128]{2,1,0:T(8,128)S(1)} %convolution_bitcast_fusion.3), kind=kOutput, calls=%fused_computation.27 | convolution fusion | flops 1358991360 | bytes 9437184 | tf_op jit(solution)/shard_map/ab,bxy->axy/dot_general | solution.py:52
  90.7 7.6 %fusion.21 = f32[96,96,128]{2,1,0:T(8,128)S(1)} fusion(f32[96,96,128]{2,0,1:T(8,128)S(1)} %get-tuple-element.21), kind=kOutput, calls=%fused_computation.33 | convolution fusion | flops 1812004864 | bytes 9437184 | tf_op jit(solution)/shard_map/dot_general | solution.py:48
  103.1 9.9 %fusion.19 = f32[96,96,128]{2,0,1:T(8,128)} fusion(f32[96,96,128]{2,1,0:T(8,128)S(1)} %convolution_bitcast_fusion.4), kind=kOutput, calls=%fused_computation.31 | convolution fusion | flops 1358991360 | bytes 9437184 | tf_op jit(solution)/shard_map/ab,bxy->axy/dot_general | solution.py:52
  113.0 7.6 %fusion.25 = f32[96,96,128]{2,1,0:T(8,128)S(1)} fusion(f32[96,96,128]{2,0,1:T(8,128)S(1)} %get-tuple-element.20), kind=kOutput, calls=%fused_computation.37 | convolution fusion | flops 1812004864 | bytes 9437184 | tf_op jit(solution)/shard_map/dot_general | solution.py:48
  120.6 6.1 convolution_bitcast_fusion.6
  126.7 6.3 copy.23
  133.0 9.0 %convolution_bitcast_fusion.2 = f32[96,96,128]{1,0,2:T(8,128)} fusion(f32[96,96,128]{1,0,2:T(8,128)} %copy.23), kind=kOutput, calls=%fused_computation.46 | convolution fusion | flops 1358991360 | bytes 9437184 | tf_op jit(solution)/shard_map/ab,zby->zay/dot_general | solution.py:49
  142.0 6.3 copy.24
  148.3 8.8 %fusion.84 = f32[96,96,128]{2,0,1:T(8,128)} fusion(f32[96,96,128]{2,0,1:T(8,128)} %copy.24), kind=kOutput, calls=%fused_computation.118 | convolution fusion | flops 1358991360 | bytes 9437184 | tf_op jit(solution)/shard_map/ab,bxy->axy/dot_general | solution.py:52
  157.0 15.5 %fusion.8 = (f32[96,1,96,128]{3,0,2,1:T(8,128)S(1)}, f32[96,1,96,128]{3,0,2,1:T(8,128)}, f32[96,1,96,128]{3,0,2,1:T(8,128)}) fusion(f32[96,96,128]{2,0,1:T(8,128)} %copy_convert_fusion), kind=kLoop, calls=%fused_computation.20 | loop fusion | flops 7077888 | bytes 18874368 | tf_op jit(solution)/shard_map/stack | solution.py:62
  172.5 22.2 %fusion.27 = (f32[]{:T(128)}, f32[96,96,128]{2,0,1:T(8,128)}) fusion(f32[96,96,128]{2,0,1:T(8,128)} %fusion.84, f32[96,96,128]{2,0,1:T(8,128)} %fusion.81, f32[96,96,128]{2,0,1:T(8,128)} %fusion.15, f32[96,96,128]{2,0,1:T(8,128)} %fusion.19, bf16[96,96,128]{2,1,0:T(8,128)(2,1)S(1)} %bitcast.111, bf16[1,96,96,128]{3,2,1,0:T(8,128)(2,1)S(1)} %copy-done, ...), kind=kOutput, calls=%fused_computation.43 | convolution fusion | flops 1384943616 | bytes 33030148 | tf_op jit(solution)/shard_map/ab,bxy->axy/dot_general | solution.py:52
  200.0 22.1 %fusion.2 = f32[96,3,96,128]{3,2,1,0:T(8,128)S(1)} fusion(f32[96,3,96,128]{3,0,2,1:T(8,128)S(1)} %maximum_multiply_fusion), kind=kOutput, calls=%fused_computation.10 | convolution fusion | flops 5435965440 | bytes 28311552 | tf_op jit(solution)/shard_map/zcxb,ba->zcxa/dot_general | solution.py:94
  222.1 15.9 %convolution_bitcast_fusion = f32[96,3,96,128]{3,2,1,0:T(8,128)} fusion(f32[96,3,96,128]{3,2,1,0:T(8,128)S(1)} %fusion.2), kind=kOutput, calls=%fused_computation.12 | convolution fusion | flops 4076946432 | bytes 28311552 | tf_op jit(solution)/shard_map/ab,zcby->zcay/dot_general | solution.py:97
  238.0 25.3 %fusion = f32[96,3,96,128]{3,0,2,1:T(8,128)S(1)} fusion(f32[96,3,96,128]{3,2,1,0:T(8,128)} %convolution_bitcast_fusion), kind=kOutput, calls=%fused_computation.8 | convolution fusion | flops 4076946432 | bytes 28311552 | tf_op jit(solution)/shard_map/ab,bcxy->acxy/dot_general | solution.py:102
  263.3 7.1 %pad_maximum_fusion = f32[96,4,96,128]{3,0,2,1:T(8,128)} fusion(f32[96,1,96,128]{3,0,2,1:T(8,128)S(1)} %bitcast.113, f32[96,3,96,128]{3,0,2,1:T(8,128)S(1)} %fusion), kind=kLoop, calls=%fused_computation.6 | loop fusion | flops 4718592 | bytes 37748736 | tf_op jit(solution)/shard_map/concatenate | solution.py:107
  270.4 15.8 %copy.35 = f32[96,4,96,128]{3,2,1,0:T(8,128)} copy(f32[96,4,96,128]{3,0,2,1:T(8,128)} %pad_maximum_fusion) | data formatting | bytes 37748736 | tf_op jit(solution)/shard_map/concatenate | solution.py:107
  286.3 218.0 %reduce-scatter.2.cloned.1.call-done = f32[3,4,96,128]{3,2,1,0:T(8,128)} async-done(((f32[96,4,96,128]{3,2,1,0:T(8,128)}), f32[3,4,96,128]{3,2,1,0:T(8,128)}) %reduce-scatter.2.cloned.1.call-update) | async-done | bytes 589840 | tf_op jit(solution)/shard_map/reduce_scatter | solution.py:106
  504.3 64.7 %psum.31 = f32[]{:T(128)} all-reduce(f32[]{:T(128)} %get-tuple-element.14), channel_id=1, replica_groups=mesh['grp'=4,'sub'=32] {'grp','sub'}, use_global_device_ids=true, to_apply=%region_7.8 | all-reduce | flops 1 | bytes 8 | tf_op jit(solution)/shard_map/psum | solution.py:115
  572.9 79.7 %all-reduce.3 = (f32[]{:T(128)}, f32[]{:T(128)}) all-reduce(f32[]{:T(128)} %multiply_reduce_fusion, f32[]{:T(128)} %multiply_reduce_fusion.1), channel_id=1, replica_groups=mesh['grp'=4,'sub'=32] {'sub'}, use_global_device_ids=true, to_apply=%region_3.4 | all-reduce | flops 2 | bytes 16 | tf_op jit(solution)/shard_map/psum | solution.py:116
  (38 shorter events, 61.5 us)
Async XLA Ops:
  9.8 47.5 %all-to-all-start = ((bf16[32,3,96,128]{3,2,1,0:T(8,128)(2,1)}), bf16[32,3,96,128]{3,2,1,0:T(8,128)(2,1)S(1)}, u32[]{:S(2)}, u32[]{:S(2)}) async-start(bf16[32,3,96,128]{3,2,1,0:T(8,128)(2,1)} %stack.10), calls=%async_computation | async-start | bytes 4718592 | tf_op jit(solution)/shard_map/all_to_all | solution.py:17
  19.4 484.8 %reduce-scatter.2.cloned.1.call-start = ((), (), s32[]{:S(2)}) async-start(), calls=%async_computation.2 | async-start | bytes 19464192 | tf_op jit(solution)/shard_map/reduce_scatter | solution.py:106
  46.9 4.7 copy-start.1
  157.0 15.5 %copy-start = (bf16[1,96,96,128]{3,2,1,0:T(8,128)(2,1)S(1)}, bf16[1,96,96,128]{3,2,1,0:T(8,128)(2,1)}, u32[]{:S(2)}) copy-start(bf16[1,96,96,128]{3,2,1,0:T(8,128)(2,1)} %param.3) | copy-start | bytes 7077892
  172.5 22.3 %copy-start.2 = (f32[96,1,96,128]{3,0,2,1:T(8,128)S(1)}, f32[96,1,96,128]{3,0,2,1:T(8,128)}, u32[]{:S(2)}) copy-start(f32[96,1,96,128]{3,0,2,1:T(8,128)} %get-tuple-element.17) | copy-start | bytes 14155780
  222.1 41.2 %slice-start = ((s8[4718592]{0:T(1024)(128)(4,1)}), s8[4194304]{0:T(1024)(128)(4,1)S(1)}, s32[]{:S(2)}) async-start(s8[4718592]{0:T(1024)(128)(4,1)} %bitcast.112), calls=%async_computation.4 | async-start | bytes 8388608
  238.0 25.3 %slice-start.1 = ((s8[4718592]{0:T(1024)(128)(4,1)}), s8[524288]{0:T(1024)(128)(4,1)S(1)}, s32[]{:S(2)}) async-start(s8[4718592]{0:T(1024)(128)(4,1)} %bitcast.112), calls=%async_computation.5 | async-start | bytes 1048576
  286.2 282.7 %all-reduce.6.cloned.1.call-start = ((), (), s32[]{:S(2)}) async-start(), calls=%async_computation.3 | async-start | bytes 1179648 | tf_op jit(solution)/shard_map/psum | solution.py:109
  654.3 8.4 %collective-permute-start = (f32[1,96,128]{2,1,0:T(8,128)S(1)}, f32[1,96,128]{2,1,0:T(8,128)S(1)}, u32[]{:S(2)}, u32[]{:S(2)}) collective-permute-start(f32[1,96,128]{2,1,0:T(8,128)S(1)} %get-tuple-element.24), channel_id=1, source_target_pairs={{1,0},{2,1},{3,2},{4,3},{5,4},{6,5},{7,6},{8,7},{9,8},{10,9},{11,1... | collective-permute-start | bytes 147464 | tf_op jit(solution)/shard_map/ppermute | solution.py:28
  656.2 10.2 %collective-permute-start.1 = (f32[1,96,128]{2,1,0:T(8,128)S(1)}, f32[1,96,128]{2,1,0:T(8,128)S(1)}, u32[]{:S(2)}, u32[]{:S(2)}) collective-permute-start(f32[1,96,128]{2,1,0:T(8,128)S(1)} %get-tuple-element.25), channel_id=1, source_target_pairs={{0,1},{1,2},{2,3},{3,4},{4,5},{5,6},{6,7},{7,8},{8,9},{9,10},{10,1... | collective-permute-start | bytes 147464 | tf_op jit(solution)/shard_map/ppermute | solution.py:27
Sparse Core Ops, SparseCore 0:
  286.3 217.8 reduce-scatter.1
  506.7 40.8 all-reduce.5
